TPU v7x, 512 devices: a whole 4x8x8 slice. The times are simulated.
512 devices in a mesh: slab: 32 (over y, x), sub: 16 (over z, core).
Axes of the slice: x: 4, y: 8, z: 8, core: 2. Of those that a mesh axis runs over, the one named last changes fastest.
Arguments:
- positions: float32 [3, 524288], P(None, 'slab'), may hold values from 0 to 129, as said below
- velocity: float32 [3, 524288], P(None, 'slab'), may hold values from -6 to 6
- density: float32 [524288], P('slab'), may hold values from 0.1 to 10
- pressure: float32 [524288], P('slab'), may hold values from 0.1 to 10
- counts: int32 [4096], P('slab'), may hold values from 8 to 128, as said below
- pair_list: int32 [3, 20480], P(None, ('slab', 'sub')), may hold values from -128 to 4095, as said below
Outputs:
- rates: float32 [5, 524288], P(None, 'slab')
Inputs may be any that keep to these rules, and one draw needn't show every extreme that they name: `positions`: particle k of leaf g lies in slab floor(g / 128) along x (x minus that index in [0, 1)), in column g mod 128 along y (likewise), and z in [0, 1). `counts`: at least 8 live particles a leaf; some leaf holds 128. `pair_list`: row 0 is a slot's home leaf, a leaf of this device's part of its slab (columns 8 * i to 8 * i + 7 on the device of index i along sub), or -1 for an empty slot. Row 1 is the other leaf, -1 for an empty slot: the home leaf itself, the leaf of the next column cyclically in the same slab, or a leaf of the next slab cyclically whose column is the home column - 1, + 0 or + 1 plus w, modulo 128; w is 0 for home leaves outside the last slab and one shift common to all pairs headed in the last slab. Row 2 is the image offset along y in units of cell width, 0 for an empty slot and for a pair of a leaf with itself; for a pair into the next slab, minus row 2 modulo 128 equals w. A leaf heads at most 5 pairs, each device holds at most 40 live slots, and some device holds exactly that many.
All inputs are finite; a program needn't handle non-finite values.
Results may differ from a plain program's by a relative error of at most 0.0003.
Values sent between devices are 32-bit elements; how exact they have to be, the bound alone decides.
A program may use at most 64 MiB of HBM per device.

v0:
```python
import math
import jax
import jax.numpy as jnp
from jax import lax
from jax.sharding import PartitionSpec as P

LEAF = 128
CAND = 5
GAMMA = 5.0 / 3.0
SUPPORT = 1.5
KERNEL_NORM = 21.0 / (2.0 * math.pi * SUPPORT**3)
MOMENT_REG = 0.05
SHEAR_SPEED = 1.0
AREA_FLOOR = 0.0001
SYM_PAIRS = ((0, 0), (0, 1), (0, 2), (1, 1), (1, 2), (2, 2))
UNIT_DIAG = (1.0, 0.0, 0.0, 1.0, 0.0, 1.0)


def shifted(shard, axis, by):
    peers = lax.axis_size(axis)
    return lax.ppermute(shard, axis, [(i, (i + by) % peers) for i in range(peers)])


def kernel(dist_sq):
    scaled = jnp.sqrt(dist_sq) / SUPPORT
    inside = jnp.maximum(1.0 - scaled, 0.0)
    return KERNEL_NORM * inside**4 * (1.0 + 4.0 * scaled)


def image_rows(tile, wrapped, offset, box_length):
    zero_row = jnp.zeros_like(offset)
    displace = jnp.stack(
        [
            wrapped * box_length,
            offset,
            zero_row,
            zero_row,
            -SHEAR_SPEED * wrapped,
            zero_row,
            zero_row,
            zero_row,
        ]
    )
    return tile + displace[:, :, None]


def sym_apply(matrix, vector):
    comp_x = matrix[0] * vector[0] + matrix[1] * vector[1] + matrix[2] * vector[2]
    comp_y = matrix[1] * vector[0] + matrix[3] * vector[1] + matrix[4] * vector[2]
    comp_z = matrix[2] * vector[0] + matrix[4] * vector[1] + matrix[5] * vector[2]
    return [comp_x, comp_y, comp_z]


def sym_inverse(matrix):
    entry_xx, entry_xy, entry_xz, entry_yy, entry_yz, entry_zz = matrix
    minor_xx = entry_yy * entry_zz - entry_yz * entry_yz
    minor_xy = entry_xz * entry_yz - entry_xy * entry_zz
    minor_xz = entry_xy * entry_yz - entry_xz * entry_yy
    minor_yy = entry_xx * entry_zz - entry_xz * entry_xz
    minor_yz = entry_xy * entry_xz - entry_xx * entry_yz
    minor_zz = entry_xx * entry_yy - entry_xy * entry_xy
    determinant = entry_xx * minor_xx + entry_xy * minor_xy + entry_xz * minor_xz
    return [
        minor / determinant
        for minor in (minor_xx, minor_xy, minor_xz, minor_yy, minor_yz, minor_zz)
    ]


def moment_tile(near_tile, far_tile, mask_near, mask_far, weight):
    separation = [
        far_tile[direction][:, None, :] - near_tile[direction][:, :, None] for direction in range(3)
    ]
    dist_sq = (
        separation[0] * separation[0]
        + separation[1] * separation[1]
        + separation[2] * separation[2]
    )
    smoothing = (
        kernel(dist_sq) * mask_near[:, :, None] * mask_far[:, None, :] * weight[:, None, None]
    )
    summands = [smoothing] + [
        smoothing * separation[left_axis] * separation[right_axis]
        for left_axis, right_axis in SYM_PAIRS
    ]
    for quantity in range(5):
        weighted = smoothing * (
            far_tile[3 + quantity][:, None, :] - near_tile[3 + quantity][:, :, None]
        )
        summands = summands + [weighted * separation[direction] for direction in range(3)]
    row_sums = jnp.stack([jnp.sum(summand, axis=2) for summand in summands])
    col_sums = jnp.stack([jnp.sum(summand, axis=1) for summand in summands])
    return (row_sums, col_sums)


def finish_moments(moments, live_mask):
    number_density = moments[0] + 1.0 - live_mask
    inverse_density = 1.0 / number_density
    second = [
        moments[1 + position] * inverse_density + MOMENT_REG * UNIT_DIAG[position]
        for position in range(6)
    ]
    inverse = sym_inverse(second)
    slopes = []
    for quantity in range(5):
        numerator = [
            moments[7 + 3 * quantity + direction] * inverse_density for direction in range(3)
        ]
        slopes = slopes + sym_apply(inverse, numerator)
    return jnp.stack([number_density] + inverse + slopes)


def side_flux(
    density_side, velocity_side, pressure_side, normal, normal_speed, lag_speed, wave_speed, contact
):
    energy = pressure_side / (GAMMA - 1.0) + 0.5 * density_side * (
        velocity_side[0] ** 2 + velocity_side[1] ** 2 + velocity_side[2] ** 2
    )
    plain_flux = [density_side * normal_speed]
    plain_flux = plain_flux + [
        density_side * velocity_side[direction] * normal_speed + pressure_side * normal[direction]
        for direction in range(3)
    ]
    plain_flux = plain_flux + [(energy + pressure_side) * normal_speed]
    conserved = (
        [density_side]
        + [density_side * velocity_side[direction] for direction in range(3)]
        + [energy]
    )
    factor = density_side * lag_speed / (wave_speed - contact)
    speed_gap = contact - normal_speed
    star_state = [factor] + [
        factor * (velocity_side[direction] + speed_gap * normal[direction])
        for direction in range(3)
    ]
    star_state = star_state + [
        factor
        * (
            energy / density_side
            + speed_gap * (contact + pressure_side / (density_side * lag_speed))
        )
    ]
    starred = [
        plain_flux[component] + wave_speed * (star_state[component] - conserved[component])
        for component in range(5)
    ]
    return (plain_flux, starred)


def hllc_flux(left_state, right_state, normal, face_vel):
    left_vel = [left_state[direction] - face_vel[direction] for direction in range(3)]
    right_vel = [right_state[direction] - face_vel[direction] for direction in range(3)]
    left_density, left_pressure = (left_state[3], left_state[4])
    right_density, right_pressure = (right_state[3], right_state[4])
    left_normal = left_vel[0] * normal[0] + left_vel[1] * normal[1] + left_vel[2] * normal[2]
    right_normal = right_vel[0] * normal[0] + right_vel[1] * normal[1] + right_vel[2] * normal[2]
    left_sound = jnp.sqrt(GAMMA * left_pressure / left_density)
    right_sound = jnp.sqrt(GAMMA * right_pressure / right_density)
    speed_left = jnp.minimum(left_normal - left_sound, right_normal - right_sound)
    speed_right = jnp.maximum(left_normal + left_sound, right_normal + right_sound)
    lag_left = speed_left - left_normal
    lag_right = speed_right - right_normal
    contact = (
        right_pressure
        - left_pressure
        + left_density * left_normal * lag_left
        - right_density * right_normal * lag_right
    ) / (left_density * lag_left - right_density * lag_right)
    flux_left, star_left = side_flux(
        left_density, left_vel, left_pressure, normal, left_normal, lag_left, speed_left, contact
    )
    flux_right, star_right = side_flux(
        right_density,
        right_vel,
        right_pressure,
        normal,
        right_normal,
        lag_right,
        speed_right,
        contact,
    )
    moving = [
        jnp.where(
            speed_left >= 0.0,
            flux_left[component],
            jnp.where(
                contact >= 0.0,
                star_left[component],
                jnp.where(speed_right >= 0.0, star_right[component], flux_right[component]),
            ),
        )
        for component in range(5)
    ]
    mass_flux = moving[0]
    momentum = [moving[1 + direction] + face_vel[direction] * mass_flux for direction in range(3)]
    face_sq = face_vel[0] ** 2 + face_vel[1] ** 2 + face_vel[2] ** 2
    energy_flux = (
        moving[4]
        + face_vel[0] * moving[1]
        + face_vel[1] * moving[2]
        + face_vel[2] * moving[3]
        + 0.5 * face_sq * mass_flux
    )
    return [mass_flux] + momentum + [energy_flux]


def flux_tile(near_tile, far_tile, near_pay, far_pay, mask_near, mask_far, weight):
    separation = [
        far_tile[direction][:, None, :] - near_tile[direction][:, :, None] for direction in range(3)
    ]
    dist_sq = (
        separation[0] * separation[0]
        + separation[1] * separation[1]
        + separation[2] * separation[2]
    )
    smoothing = kernel(dist_sq) * mask_near[:, :, None] * mask_far[:, None, :]
    near_density = near_pay[0][:, :, None]
    far_density = far_pay[0][:, None, :]
    near_matrix = [near_pay[1 + position][:, :, None] for position in range(6)]
    far_matrix = [far_pay[1 + position][:, None, :] for position in range(6)]
    toward_near = sym_apply(near_matrix, separation)
    toward_far = sym_apply(far_matrix, separation)
    near_scale = smoothing / (near_density * near_density)
    far_scale = smoothing / (far_density * far_density)
    area = [
        near_scale * toward_near[direction] + far_scale * toward_far[direction]
        for direction in range(3)
    ]
    magnitude = jnp.sqrt(area[0] * area[0] + area[1] * area[1] + area[2] * area[2])
    clamp_scale = 1.0 / jnp.maximum(magnitude, AREA_FLOOR)
    normal = [area[direction] * clamp_scale for direction in range(3)]
    left_state = []
    right_state = []
    for quantity in range(5):
        near_value = near_tile[3 + quantity][:, :, None]
        far_value = far_tile[3 + quantity][:, None, :]
        near_change = 0.5 * (
            near_pay[7 + 3 * quantity][:, :, None] * separation[0]
            + near_pay[8 + 3 * quantity][:, :, None] * separation[1]
            + near_pay[9 + 3 * quantity][:, :, None] * separation[2]
        )
        far_change = 0.5 * (
            far_pay[7 + 3 * quantity][:, None, :] * separation[0]
            + far_pay[8 + 3 * quantity][:, None, :] * separation[1]
            + far_pay[9 + 3 * quantity][:, None, :] * separation[2]
        )
        low_bound = jnp.minimum(near_value, far_value)
        high_bound = jnp.maximum(near_value, far_value)
        left_state.append(jnp.clip(near_value + near_change, low_bound, high_bound))
        right_state.append(jnp.clip(far_value - far_change, low_bound, high_bound))
    face_vel = [
        0.5 * (near_tile[3 + direction][:, :, None] + far_tile[3 + direction][:, None, :])
        for direction in range(3)
    ]
    fluxes = hllc_flux(left_state, right_state, normal, face_vel)
    pair_scale = magnitude * weight[:, None, None]
    row_sums = jnp.stack([-jnp.sum(pair_scale * face_flux, axis=2) for face_flux in fluxes])
    col_sums = jnp.stack([jnp.sum(pair_scale * face_flux, axis=1) for face_flux in fluxes])
    return (row_sums, col_sums)


def shards(positions, velocity, density, pressure, counts, pair_list):
    slab_leaves = counts.shape[0]
    slab_count = lax.axis_size("slab")
    slab_index = lax.axis_index("slab")
    state = jnp.concatenate([positions, velocity, density[None], pressure[None]], axis=0)
    upper_state, upper_counts = shifted((state, counts.astype(jnp.float32)), "slab", -1)
    slab_state = state.reshape(8, slab_leaves, LEAF)
    upper_slab = upper_state.reshape(8, slab_leaves, LEAF)
    upper_whole = upper_counts.astype(jnp.int32)
    box_length = jnp.asarray(slab_count, jnp.float32)
    slot_count = pair_list.shape[1]
    ranking = jnp.argsort((pair_list[0] < 0).astype(jnp.int32), stable=True)
    slots = pair_list[:, ranking]
    live_count = jnp.sum((pair_list[0] >= 0).astype(jnp.int32))
    occupied = slots[0] >= 0
    home_leaf = jnp.where(occupied, slots[0], 0)
    other_leaf = jnp.where(occupied, slots[1], 0)
    wrapped = (other_leaf // slab_leaves < home_leaf // slab_leaves).astype(jnp.float32)
    offset = slots[2].astype(jnp.float32)
    weight = jnp.where(occupied, jnp.where(home_leaf == other_leaf, 0.5, 1.0), 0.0).astype(
        jnp.float32
    )
    base_leaf = slab_index * slab_leaves
    turns = (live_count + CAND - 1) // CAND
    window = jnp.concatenate([slab_state, upper_slab], axis=1)
    window_counts = jnp.concatenate([counts, upper_whole])
    width = 2 * slab_leaves
    home_window = jnp.where(occupied, home_leaf - base_leaf, 0)
    other_window = jnp.where(occupied, (other_leaf - base_leaf) % (slab_count * slab_leaves), 0)
    window_mask = (jnp.arange(LEAF, dtype=jnp.int32)[None, :] < window_counts[:, None]).astype(
        jnp.float32
    )
    leaf_ids = jnp.arange(width, dtype=jnp.int32)
    home_hot = (home_window[:, None] == leaf_ids[None, :]).astype(jnp.float32)
    other_hot = (other_window[:, None] == leaf_ids[None, :]).astype(jnp.float32)

    def sweep(tile_fn, row_count):

        def one_turn(turn_index, buffers):
            row_buffer, col_buffer = buffers
            first_slot = turn_index * CAND
            home_part = lax.dynamic_slice_in_dim(home_window, first_slot, CAND)
            other_part = lax.dynamic_slice_in_dim(other_window, first_slot, CAND)
            wrap_part = lax.dynamic_slice_in_dim(wrapped, first_slot, CAND)
            offset_part = lax.dynamic_slice_in_dim(offset, first_slot, CAND)
            weight_part = lax.dynamic_slice_in_dim(weight, first_slot, CAND)
            row_sums, col_sums = tile_fn(home_part, other_part, wrap_part, offset_part, weight_part)
            row_buffer = lax.dynamic_update_slice_in_dim(row_buffer, row_sums, first_slot, 1)
            col_buffer = lax.dynamic_update_slice_in_dim(col_buffer, col_sums, first_slot, 1)
            return (row_buffer, col_buffer)

        empty = jnp.zeros((row_count, slot_count, LEAF), jnp.float32)
        row_buffer, col_buffer = lax.fori_loop(0, turns, one_turn, (empty, empty))
        total = jnp.einsum("rsp,sw->rwp", row_buffer, home_hot, precision=lax.Precision.HIGHEST)
        return total + jnp.einsum(
            "rsp,sw->rwp", col_buffer, other_hot, precision=lax.Precision.HIGHEST
        )

    def settle(partial_value):
        row_count = partial_value.shape[0]
        partial_value = lax.psum(partial_value, "sub")
        own_part = partial_value[:, :slab_leaves]
        next_part = partial_value[:, slab_leaves:]
        returned = shifted(next_part, "slab", 1)
        merged = own_part + returned
        return merged

    def moment_fn(home_part, other_part, wrap_part, offset_part, weight_part):
        near_tile = jnp.take(window, home_part, axis=1)
        far_tile = image_rows(
            jnp.take(window, other_part, axis=1), wrap_part, offset_part, box_length
        )
        return moment_tile(
            near_tile, far_tile, window_mask[home_part], window_mask[other_part], weight_part
        )

    moments = settle(sweep(moment_fn, 22))
    own_count = moments.shape[1]
    payload = finish_moments(moments, window_mask[:own_count])
    arrived = shifted(payload, "slab", -1)
    window_payload = jnp.concatenate([payload, arrived], axis=1)

    def flux_fn(home_part, other_part, wrap_part, offset_part, weight_part):
        near_tile = jnp.take(window, home_part, axis=1)
        far_tile = image_rows(
            jnp.take(window, other_part, axis=1), wrap_part, offset_part, box_length
        )
        near_pay = jnp.take(window_payload, home_part, axis=1)
        far_pay = jnp.take(window_payload, other_part, axis=1)
        return flux_tile(
            near_tile,
            far_tile,
            near_pay,
            far_pay,
            window_mask[home_part],
            window_mask[other_part],
            weight_part,
        )

    flux_sum = settle(sweep(flux_fn, 5))
    rate_part = (payload[0][None] * flux_sum).reshape(5, own_count * LEAF)
    return rate_part


def solution(mesh):
    placed = (
        P(None, "slab"),
        P(None, "slab"),
        P("slab"),
        P("slab"),
        P("slab"),
        P(None, ("slab", "sub")),
    )
    return jax.shard_map(
        shards, mesh=mesh, in_specs=placed, out_specs=P(None, "slab"), check_vma=False
    )
```

profile of v0, /device:TPU:1, one launch (start us, length us, event | category | flops | bytes accessed | tf_op | source)
XLA Modules:
  0.0 1030.1 jit_solution(6164458053880758125)
XLA Ops:
  7.3 8.1 collective-permute-start.1
  16.7 2.5 collective-permute-start
  22.6 2.0 sort.17
  28.0 3.1 collective-permute-done
  32.4 74.5 %while.30 = (s32[]{:T(128)}, f32[22,40,128]{2,1,0:T(8,128)S(1)}, f32[22,40,128]{2,1,0:T(8,128)S(1)}, s32[]{:T(128)}, s32[40]{0:T(128)}, /*index=5*/f32[8,256,128...) while((s32[]{:T(128)}, f32[22,40,128]{2,1,0:T(8,128)S(1)}, ...), condition=%wide.region_47.49_spmd.clone, body=%wide.region_2.48_spmd.clone.sunk | while | flops 9721420 | bytes 1241347 | solution.py:313
  37.0 2.9 fusion.246
  46.4 2.9 fusion.246
  55.7 2.9 fusion.246
  65.0 2.9 fusion.246
  74.3 2.9 fusion.246
  83.6 2.9 fusion.246
  92.9 2.9 fusion.246
  102.3 2.9 fusion.246
  108.9 3.9 add_bitcast_fusion
  112.9 126.5 %all-reduce.3.cloned.1.call-done = f32[22,256,128]{2,1,0:T(8,128)} async-done(((f32[22,256,128]{2,1,0:T(8,128)}), f32[22,256,128]{2,1,0:T(8,128)}) %all-reduce.3.cloned.1.call-update) | async-done | bytes 2883600 | tf_op jit(solution)/shard_map/psum | solution.py:321
  240.9 3.1 collective-permute-start.2
  244.1 34.1 %collective-permute-done.2 = f32[22,128,128]{2,1,0:T(8,128)S(1)} collective-permute-done((f32[22,128,128]{2,1,0:T(8,128)S(1)}, f32[22,128,128]{2,1,0:T(8,128)S(1)}, u32[]{:S(2)}, u32[]{:S(2)}) %collective-permute-start.2) | collective-permute-done | bytes 1441824 | tf_op jit(solution)/shard_map/ppermute | solution.py:21
  279.4 3.4 collective-permute-start.3
  282.8 29.6 %collective-permute-done.3 = f32[22,128,128]{2,1,0:T(8,128)S(1)} collective-permute-done((f32[22,128,128]{2,1,0:T(8,128)S(1)}, f32[22,128,128]{2,1,0:T(8,128)S(1)}, u32[]{:S(2)}, u32[]{:S(2)}) %collective-permute-start.3) | collective-permute-done | bytes 1441824 | tf_op jit(solution)/shard_map/ppermute | solution.py:21
  315.0 570.6 %while.31 = (s32[]{:T(128)}, f32[5,40,128]{2,1,0:T(8,128)}, f32[5,40,128]{2,1,0:T(8,128)S(1)}, s32[]{:T(128)}, s32[40]{0:T(128)}, /*index=5*/f32[8,256,128]{2,0,...) while((s32[]{:T(128)}, f32[5,40,128]{2,1,0:T(8,128)}, ...), condition=%wide.region_60.63_spmd.clone, body=%wide.region_49.62_spmd.clone.sunk | while | flops 113486544 | bytes 2761233 | solution.py:313
  353.4 6.3 fusion.254
  359.8 5.9 fusion.253
  365.7 6.3 fusion.255
  372.3 5.6 fusion.256
  377.9 6.8 fusion.257
  424.7 6.3 fusion.254
  431.1 5.9 fusion.253
  437.0 6.3 fusion.255
  443.6 5.6 fusion.256
  449.3 6.8 fusion.257
  496.0 6.3 fusion.254
  502.4 5.9 fusion.253
  508.3 6.3 fusion.255
  514.9 5.6 fusion.256
  520.6 6.8 fusion.257
  567.3 6.3 fusion.254
  573.7 5.9 fusion.253
  579.7 6.3 fusion.255
  586.2 5.6 fusion.256
  591.9 6.8 fusion.257
  638.7 6.3 fusion.254
  645.0 5.9 fusion.253
  651.0 6.3 fusion.255
  657.6 5.6 fusion.256
  663.2 6.8 fusion.257
  710.0 6.3 fusion.254
  716.4 5.9 fusion.253
  722.3 6.3 fusion.255
  728.9 5.6 fusion.256
  734.5 6.8 fusion.257
  781.3 6.3 fusion.254
  787.7 5.9 fusion.253
  793.6 6.3 fusion.255
  800.2 5.6 fusion.256
  805.9 6.8 fusion.257
  852.6 6.3 fusion.254
  859.0 5.9 fusion.253
  864.9 6.3 fusion.255
  871.5 5.6 fusion.256
  877.2 6.8 fusion.257
  887.0 2.1 fusion.153
  889.1 117.4 %all-reduce.5.cloned.1.call-done = f32[5,256,128]{2,1,0:T(8,128)} async-done(((f32[5,256,128]{2,1,0:T(8,128)}), f32[5,256,128]{2,1,0:T(8,128)}) %all-reduce.5.cloned.1.call-update) | async-done | bytes 655376 | tf_op jit(solution)/shard_map/psum | solution.py:321
  1007.5 3.1 collective-permute-start.4
  1010.6 10.7 %collective-permute-done.4 = f32[5,128,128]{2,1,0:T(8,128)S(1)} collective-permute-done((f32[5,128,128]{2,1,0:T(8,128)S(1)}, f32[5,128,128]{2,1,0:T(8,128)S(1)}, u32[]{:S(2)}, u32[]{:S(2)}) %collective-permute-start.4) | collective-permute-done | bytes 327712 | tf_op jit(solution)/shard_map/ppermute | solution.py:21
  (2204 shorter events, 384.3 us)
Async XLA Ops:
  6.5 232.8 %all-reduce.3.cloned.1.call-start = ((), (), s32[]{:S(2)}) async-start(), calls=%async_computation | async-start | bytes 5767168 | tf_op jit(solution)/shard_map/psum | solution.py:321
  7.3 20.1 %collective-permute-start.1 = (f32[128]{0:T(128)S(1)}, f32[128]{0:T(128)S(1)}, u32[]{:S(2)}, u32[]{:S(2)}) collective-permute-start(f32[128]{0:T(128)S(1)} %convert_element_type.36), channel_id=1, source_target_pairs={{0,496},{16,0},{32,16},{48,32},{64,48},{80,64},{96,80},{112,96},{1... | collective-permute-start | bytes 1544 | tf_op jit(solution)/shard_map/ppermute | solution.py:21
  16.7 14.4 %collective-permute-start = (f32[8,16384]{1,0:T(8,128)S(1)}, f32[8,16384]{1,0:T(8,128)S(1)}, u32[]{:S(2)}, u32[]{:S(2)}) collective-permute-start(f32[8,16384]{1,0:T(8,128)S(1)} %pad_maximum_fusion.2), channel_id=1, source_target_pairs={{0,496},{16,0},{32,16},{48,32},{64,48},{80,64},{96,80},{112,96},{1... | collective-permute-start | bytes 1572872 | tf_op jit(solution)/shard_map/ppermute | solution.py:21
  112.8 893.7 %all-reduce.5.cloned.1.call-start = ((), (), s32[]{:S(2)}) async-start(), calls=%async_computation.1 | async-start | bytes 1310720 | tf_op jit(solution)/shard_map/psum | solution.py:321
  239.3 38.8 %copy-start = (f32[22,256,128]{2,1,0:T(8,128)S(1)}, f32[22,256,128]{2,1,0:T(8,128)}, u32[]{:S(2)}) copy-start(f32[22,256,128]{2,1,0:T(8,128)} %all-reduce.3.cloned.1.call-done) | copy-start | bytes 8650756
  240.9 37.2 %collective-permute-start.2 = (f32[22,128,128]{2,1,0:T(8,128)S(1)}, f32[22,128,128]{2,1,0:T(8,128)S(1)}, u32[]{:S(2)}, u32[]{:S(2)}) collective-permute-start(f32[22,128,128]{2,1,0:T(8,128)S(1)} %slice.766), channel_id=1, source_target_pairs={{0,16},{16,32},{32,48},{48,64},{64,80},{80,96},{96,112},{112,128},... | collective-permute-start | bytes 4325384 | tf_op jit(solution)/shard_map/ppermute | solution.py:21
  279.4 33.0 %collective-permute-start.3 = (f32[22,128,128]{2,1,0:T(8,128)S(1)}, f32[22,128,128]{2,1,0:T(8,128)S(1)}, u32[]{:S(2)}, u32[]{:S(2)}) collective-permute-start(f32[22,128,128]{2,1,0:T(8,128)S(1)} %bitcast_dynamic-update-slice_fusion), channel_id=1, source_target_pairs={{0,496},{16,0},{32,16},{48,32},{64,48},{80,64},{96,80},{112,96},{1... | collective-permute-start | bytes 4325384 | tf_op jit(solution)/shard_map/ppermute | solution.py:21
  330.8 28.8 %copy-start.6 = (f32[1,5,128]{2,1,0:T(8,128)S(1)}, f32[1,5,128]{2,1,0:T(8,128)}, u32[]{:S(2)}) copy-start(f32[1,5,128]{2,1,0:T(8,128)} %copy.379) | copy-start | bytes 7684 | tf_op jit(solution)/shard_map/while
  330.8 28.8 %copy-start.7 = (f32[1,5,128]{2,1,0:T(8,128)S(1)}, f32[1,5,128]{2,1,0:T(8,128)}, u32[]{:S(2)}) copy-start(f32[1,5,128]{2,1,0:T(8,128)} %copy.380) | copy-start | bytes 7684 | tf_op jit(solution)/shard_map/while
  330.9 28.8 %copy-start.8 = (f32[1,5,128]{2,1,0:T(8,128)S(1)}, f32[1,5,128]{2,1,0:T(8,128)}, u32[]{:S(2)}) copy-start(f32[1,5,128]{2,1,0:T(8,128)} %copy.381) | copy-start | bytes 7684 | tf_op jit(solution)/shard_map/while
  330.9 28.8 %copy-start.9 = (f32[1,5,128]{2,1,0:T(8,128)S(1)}, f32[1,5,128]{2,1,0:T(8,128)}, u32[]{:S(2)}) copy-start(f32[1,5,128]{2,1,0:T(8,128)} %copy.384) | copy-start | bytes 7684 | tf_op jit(solution)/shard_map/while
  330.9 28.8 %copy-start.10 = (f32[1,5,128]{2,1,0:T(8,128)S(1)}, f32[1,5,128]{2,1,0:T(8,128)}, u32[]{:S(2)}) copy-start(f32[1,5,128]{2,1,0:T(8,128)} %copy.385) | copy-start | bytes 7684 | tf_op jit(solution)/shard_map/while
  330.9 28.8 %copy-start.12 = (f32[1,5,128]{2,1,0:T(8,128)S(1)}, f32[1,5,128]{2,1,0:T(8,128)}, u32[]{:S(2)}) copy-start(f32[1,5,128]{2,1,0:T(8,128)} %copy.386) | copy-start | bytes 7684 | tf_op jit(solution)/shard_map/while
  344.7 33.2 %copy-start.11 = (f32[1,5,128]{2,1,0:T(8,128)S(1)}, f32[1,5,128]{2,1,0:T(8,128)}, u32[]{:S(2)}) copy-start(f32[1,5,128]{2,1,0:T(8,128)} %copy.385) | copy-start | bytes 7684 | tf_op jit(solution)/shard_map/while
  402.2 28.8 %copy-start.6 = (f32[1,5,128]{2,1,0:T(8,128)S(1)}, f32[1,5,128]{2,1,0:T(8,128)}, u32[]{:S(2)}) copy-start(f32[1,5,128]{2,1,0:T(8,128)} %copy.379) | copy-start | bytes 7684 | tf_op jit(solution)/shard_map/while
  402.2 28.8 %copy-start.7 = (f32[1,5,128]{2,1,0:T(8,128)S(1)}, f32[1,5,128]{2,1,0:T(8,128)}, u32[]{:S(2)}) copy-start(f32[1,5,128]{2,1,0:T(8,128)} %copy.380) | copy-start | bytes 7684 | tf_op jit(solution)/shard_map/while
  402.2 28.8 %copy-start.8 = (f32[1,5,128]{2,1,0:T(8,128)S(1)}, f32[1,5,128]{2,1,0:T(8,128)}, u32[]{:S(2)}) copy-start(f32[1,5,128]{2,1,0:T(8,128)} %copy.381) | copy-start | bytes 7684 | tf_op jit(solution)/shard_map/while
  402.2 28.8 %copy-start.9 = (f32[1,5,128]{2,1,0:T(8,128)S(1)}, f32[1,5,128]{2,1,0:T(8,128)}, u32[]{:S(2)}) copy-start(f32[1,5,128]{2,1,0:T(8,128)} %copy.384) | copy-start | bytes 7684 | tf_op jit(solution)/shard_map/while
  402.2 28.8 %copy-start.10 = (f32[1,5,128]{2,1,0:T(8,128)S(1)}, f32[1,5,128]{2,1,0:T(8,128)}, u32[]{:S(2)}) copy-start(f32[1,5,128]{2,1,0:T(8,128)} %copy.385) | copy-start | bytes 7684 | tf_op jit(solution)/shard_map/while
  402.2 28.8 %copy-start.12 = (f32[1,5,128]{2,1,0:T(8,128)S(1)}, f32[1,5,128]{2,1,0:T(8,128)}, u32[]{:S(2)}) copy-start(f32[1,5,128]{2,1,0:T(8,128)} %copy.386) | copy-start | bytes 7684 | tf_op jit(solution)/shard_map/while
  416.0 33.2 %copy-start.11 = (f32[1,5,128]{2,1,0:T(8,128)S(1)}, f32[1,5,128]{2,1,0:T(8,128)}, u32[]{:S(2)}) copy-start(f32[1,5,128]{2,1,0:T(8,128)} %copy.385) | copy-start | bytes 7684 | tf_op jit(solution)/shard_map/while
  473.5 28.8 %copy-start.6 = (f32[1,5,128]{2,1,0:T(8,128)S(1)}, f32[1,5,128]{2,1,0:T(8,128)}, u32[]{:S(2)}) copy-start(f32[1,5,128]{2,1,0:T(8,128)} %copy.379) | copy-start | bytes 7684 | tf_op jit(solution)/shard_map/while
  473.5 28.8 %copy-start.7 = (f32[1,5,128]{2,1,0:T(8,128)S(1)}, f32[1,5,128]{2,1,0:T(8,128)}, u32[]{:S(2)}) copy-start(f32[1,5,128]{2,1,0:T(8,128)} %copy.380) | copy-start | bytes 7684 | tf_op jit(solution)/shard_map/while
  473.5 28.8 %copy-start.8 = (f32[1,5,128]{2,1,0:T(8,128)S(1)}, f32[1,5,128]{2,1,0:T(8,128)}, u32[]{:S(2)}) copy-start(f32[1,5,128]{2,1,0:T(8,128)} %copy.381) | copy-start | bytes 7684 | tf_op jit(solution)/shard_map/while
  473.5 28.8 %copy-start.9 = (f32[1,5,128]{2,1,0:T(8,128)S(1)}, f32[1,5,128]{2,1,0:T(8,128)}, u32[]{:S(2)}) copy-start(f32[1,5,128]{2,1,0:T(8,128)} %copy.384) | copy-start | bytes 7684 | tf_op jit(solution)/shard_map/while
  473.5 28.8 %copy-start.10 = (f32[1,5,128]{2,1,0:T(8,128)S(1)}, f32[1,5,128]{2,1,0:T(8,128)}, u32[]{:S(2)}) copy-start(f32[1,5,128]{2,1,0:T(8,128)} %copy.385) | copy-start | bytes 7684 | tf_op jit(solution)/shard_map/while
  473.5 28.8 %copy-start.12 = (f32[1,5,128]{2,1,0:T(8,128)S(1)}, f32[1,5,128]{2,1,0:T(8,128)}, u32[]{:S(2)}) copy-start(f32[1,5,128]{2,1,0:T(8,128)} %copy.386) | copy-start | bytes 7684 | tf_op jit(solution)/shard_map/while
  487.3 33.2 %copy-start.11 = (f32[1,5,128]{2,1,0:T(8,128)S(1)}, f32[1,5,128]{2,1,0:T(8,128)}, u32[]{:S(2)}) copy-start(f32[1,5,128]{2,1,0:T(8,128)} %copy.385) | copy-start | bytes 7684 | tf_op jit(solution)/shard_map/while
  544.8 28.8 %copy-start.6 = (f32[1,5,128]{2,1,0:T(8,128)S(1)}, f32[1,5,128]{2,1,0:T(8,128)}, u32[]{:S(2)}) copy-start(f32[1,5,128]{2,1,0:T(8,128)} %copy.379) | copy-start | bytes 7684 | tf_op jit(solution)/shard_map/while
  544.8 28.8 %copy-start.7 = (f32[1,5,128]{2,1,0:T(8,128)S(1)}, f32[1,5,128]{2,1,0:T(8,128)}, u32[]{:S(2)}) copy-start(f32[1,5,128]{2,1,0:T(8,128)} %copy.380) | copy-start | bytes 7684 | tf_op jit(solution)/shard_map/while
  544.8 28.8 %copy-start.8 = (f32[1,5,128]{2,1,0:T(8,128)S(1)}, f32[1,5,128]{2,1,0:T(8,128)}, u32[]{:S(2)}) copy-start(f32[1,5,128]{2,1,0:T(8,128)} %copy.381) | copy-start | bytes 7684 | tf_op jit(solution)/shard_map/while
  544.8 28.8 %copy-start.9 = (f32[1,5,128]{2,1,0:T(8,128)S(1)}, f32[1,5,128]{2,1,0:T(8,128)}, u32[]{:S(2)}) copy-start(f32[1,5,128]{2,1,0:T(8,128)} %copy.384) | copy-start | bytes 7684 | tf_op jit(solution)/shard_map/while
  544.8 28.8 %copy-start.10 = (f32[1,5,128]{2,1,0:T(8,128)S(1)}, f32[1,5,128]{2,1,0:T(8,128)}, u32[]{:S(2)}) copy-start(f32[1,5,128]{2,1,0:T(8,128)} %copy.385) | copy-start | bytes 7684 | tf_op jit(solution)/shard_map/while
  544.9 28.8 %copy-start.12 = (f32[1,5,128]{2,1,0:T(8,128)S(1)}, f32[1,5,128]{2,1,0:T(8,128)}, u32[]{:S(2)}) copy-start(f32[1,5,128]{2,1,0:T(8,128)} %copy.386) | copy-start | bytes 7684 | tf_op jit(solution)/shard_map/while
  558.6 33.2 %copy-start.11 = (f32[1,5,128]{2,1,0:T(8,128)S(1)}, f32[1,5,128]{2,1,0:T(8,128)}, u32[]{:S(2)}) copy-start(f32[1,5,128]{2,1,0:T(8,128)} %copy.385) | copy-start | bytes 7684 | tf_op jit(solution)/shard_map/while
  616.1 28.8 %copy-start.6 = (f32[1,5,128]{2,1,0:T(8,128)S(1)}, f32[1,5,128]{2,1,0:T(8,128)}, u32[]{:S(2)}) copy-start(f32[1,5,128]{2,1,0:T(8,128)} %copy.379) | copy-start | bytes 7684 | tf_op jit(solution)/shard_map/while
  616.1 28.8 %copy-start.7 = (f32[1,5,128]{2,1,0:T(8,128)S(1)}, f32[1,5,128]{2,1,0:T(8,128)}, u32[]{:S(2)}) copy-start(f32[1,5,128]{2,1,0:T(8,128)} %copy.380) | copy-start | bytes 7684 | tf_op jit(solution)/shard_map/while
  616.1 28.8 %copy-start.8 = (f32[1,5,128]{2,1,0:T(8,128)S(1)}, f32[1,5,128]{2,1,0:T(8,128)}, u32[]{:S(2)}) copy-start(f32[1,5,128]{2,1,0:T(8,128)} %copy.381) | copy-start | bytes 7684 | tf_op jit(solution)/shard_map/while
  616.2 28.8 %copy-start.9 = (f32[1,5,128]{2,1,0:T(8,128)S(1)}, f32[1,5,128]{2,1,0:T(8,128)}, u32[]{:S(2)}) copy-start(f32[1,5,128]{2,1,0:T(8,128)} %copy.384) | copy-start | bytes 7684 | tf_op jit(solution)/shard_map/while
  616.2 28.8 %copy-start.10 = (f32[1,5,128]{2,1,0:T(8,128)S(1)}, f32[1,5,128]{2,1,0:T(8,128)}, u32[]{:S(2)}) copy-start(f32[1,5,128]{2,1,0:T(8,128)} %copy.385) | copy-start | bytes 7684 | tf_op jit(solution)/shard_map/while
  616.2 28.8 %copy-start.12 = (f32[1,5,128]{2,1,0:T(8,128)S(1)}, f32[1,5,128]{2,1,0:T(8,128)}, u32[]{:S(2)}) copy-start(f32[1,5,128]{2,1,0:T(8,128)} %copy.386) | copy-start | bytes 7684 | tf_op jit(solution)/shard_map/while
  630.0 33.2 %copy-start.11 = (f32[1,5,128]{2,1,0:T(8,128)S(1)}, f32[1,5,128]{2,1,0:T(8,128)}, u32[]{:S(2)}) copy-start(f32[1,5,128]{2,1,0:T(8,128)} %copy.385) | copy-start | bytes 7684 | tf_op jit(solution)/shard_map/while
  687.4 28.8 %copy-start.6 = (f32[1,5,128]{2,1,0:T(8,128)S(1)}, f32[1,5,128]{2,1,0:T(8,128)}, u32[]{:S(2)}) copy-start(f32[1,5,128]{2,1,0:T(8,128)} %copy.379) | copy-start | bytes 7684 | tf_op jit(solution)/shard_map/while
  687.5 28.8 %copy-start.7 = (f32[1,5,128]{2,1,0:T(8,128)S(1)}, f32[1,5,128]{2,1,0:T(8,128)}, u32[]{:S(2)}) copy-start(f32[1,5,128]{2,1,0:T(8,128)} %copy.380) | copy-start | bytes 7684 | tf_op jit(solution)/shard_map/while
  687.5 28.8 %copy-start.8 = (f32[1,5,128]{2,1,0:T(8,128)S(1)}, f32[1,5,128]{2,1,0:T(8,128)}, u32[]{:S(2)}) copy-start(f32[1,5,128]{2,1,0:T(8,128)} %copy.381) | copy-start | bytes 7684 | tf_op jit(solution)/shard_map/while
  687.5 28.8 %copy-start.9 = (f32[1,5,128]{2,1,0:T(8,128)S(1)}, f32[1,5,128]{2,1,0:T(8,128)}, u32[]{:S(2)}) copy-start(f32[1,5,128]{2,1,0:T(8,128)} %copy.384) | copy-start | bytes 7684 | tf_op jit(solution)/shard_map/while
  687.5 28.8 %copy-start.10 = (f32[1,5,128]{2,1,0:T(8,128)S(1)}, f32[1,5,128]{2,1,0:T(8,128)}, u32[]{:S(2)}) copy-start(f32[1,5,128]{2,1,0:T(8,128)} %copy.385) | copy-start | bytes 7684 | tf_op jit(solution)/shard_map/while
  687.5 28.8 %copy-start.12 = (f32[1,5,128]{2,1,0:T(8,128)S(1)}, f32[1,5,128]{2,1,0:T(8,128)}, u32[]{:S(2)}) copy-start(f32[1,5,128]{2,1,0:T(8,128)} %copy.386) | copy-start | bytes 7684 | tf_op jit(solution)/shard_map/while
  701.3 33.2 %copy-start.11 = (f32[1,5,128]{2,1,0:T(8,128)S(1)}, f32[1,5,128]{2,1,0:T(8,128)}, u32[]{:S(2)}) copy-start(f32[1,5,128]{2,1,0:T(8,128)} %copy.385) | copy-start | bytes 7684 | tf_op jit(solution)/shard_map/while
  758.8 28.8 %copy-start.6 = (f32[1,5,128]{2,1,0:T(8,128)S(1)}, f32[1,5,128]{2,1,0:T(8,128)}, u32[]{:S(2)}) copy-start(f32[1,5,128]{2,1,0:T(8,128)} %copy.379) | copy-start | bytes 7684 | tf_op jit(solution)/shard_map/while
  758.8 28.8 %copy-start.7 = (f32[1,5,128]{2,1,0:T(8,128)S(1)}, f32[1,5,128]{2,1,0:T(8,128)}, u32[]{:S(2)}) copy-start(f32[1,5,128]{2,1,0:T(8,128)} %copy.380) | copy-start | bytes 7684 | tf_op jit(solution)/shard_map/while
  758.8 28.8 %copy-start.8 = (f32[1,5,128]{2,1,0:T(8,128)S(1)}, f32[1,5,128]{2,1,0:T(8,128)}, u32[]{:S(2)}) copy-start(f32[1,5,128]{2,1,0:T(8,128)} %copy.381) | copy-start | bytes 7684 | tf_op jit(solution)/shard_map/while
  758.8 28.8 %copy-start.9 = (f32[1,5,128]{2,1,0:T(8,128)S(1)}, f32[1,5,128]{2,1,0:T(8,128)}, u32[]{:S(2)}) copy-start(f32[1,5,128]{2,1,0:T(8,128)} %copy.384) | copy-start | bytes 7684 | tf_op jit(solution)/shard_map/while
  758.8 28.8 %copy-start.10 = (f32[1,5,128]{2,1,0:T(8,128)S(1)}, f32[1,5,128]{2,1,0:T(8,128)}, u32[]{:S(2)}) copy-start(f32[1,5,128]{2,1,0:T(8,128)} %copy.385) | copy-start | bytes 7684 | tf_op jit(solution)/shard_map/while
  758.8 28.8 %copy-start.12 = (f32[1,5,128]{2,1,0:T(8,128)S(1)}, f32[1,5,128]{2,1,0:T(8,128)}, u32[]{:S(2)}) copy-start(f32[1,5,128]{2,1,0:T(8,128)} %copy.386) | copy-start | bytes 7684 | tf_op jit(solution)/shard_map/while
  772.6 33.2 %copy-start.11 = (f32[1,5,128]{2,1,0:T(8,128)S(1)}, f32[1,5,128]{2,1,0:T(8,128)}, u32[]{:S(2)}) copy-start(f32[1,5,128]{2,1,0:T(8,128)} %copy.385) | copy-start | bytes 7684 | tf_op jit(solution)/shard_map/while
  830.1 28.8 %copy-start.6 = (f32[1,5,128]{2,1,0:T(8,128)S(1)}, f32[1,5,128]{2,1,0:T(8,128)}, u32[]{:S(2)}) copy-start(f32[1,5,128]{2,1,0:T(8,128)} %copy.379) | copy-start | bytes 7684 | tf_op jit(solution)/shard_map/while
  830.1 28.8 %copy-start.7 = (f32[1,5,128]{2,1,0:T(8,128)S(1)}, f32[1,5,128]{2,1,0:T(8,128)}, u32[]{:S(2)}) copy-start(f32[1,5,128]{2,1,0:T(8,128)} %copy.380) | copy-start | bytes 7684 | tf_op jit(solution)/shard_map/while
  830.1 28.8 %copy-start.8 = (f32[1,5,128]{2,1,0:T(8,128)S(1)}, f32[1,5,128]{2,1,0:T(8,128)}, u32[]{:S(2)}) copy-start(f32[1,5,128]{2,1,0:T(8,128)} %copy.381) | copy-start | bytes 7684 | tf_op jit(solution)/shard_map/while
  830.1 28.8 %copy-start.9 = (f32[1,5,128]{2,1,0:T(8,128)S(1)}, f32[1,5,128]{2,1,0:T(8,128)}, u32[]{:S(2)}) copy-start(f32[1,5,128]{2,1,0:T(8,128)} %copy.384) | copy-start | bytes 7684 | tf_op jit(solution)/shard_map/while
  830.1 28.8 %copy-start.10 = (f32[1,5,128]{2,1,0:T(8,128)S(1)}, f32[1,5,128]{2,1,0:T(8,128)}, u32[]{:S(2)}) copy-start(f32[1,5,128]{2,1,0:T(8,128)} %copy.385) | copy-start | bytes 7684 | tf_op jit(solution)/shard_map/while
  830.1 28.8 %copy-start.12 = (f32[1,5,128]{2,1,0:T(8,128)S(1)}, f32[1,5,128]{2,1,0:T(8,128)}, u32[]{:S(2)}) copy-start(f32[1,5,128]{2,1,0:T(8,128)} %copy.386) | copy-start | bytes 7684 | tf_op jit(solution)/shard_map/while
  843.9 33.2 %copy-start.11 = (f32[1,5,128]{2,1,0:T(8,128)S(1)}, f32[1,5,128]{2,1,0:T(8,128)}, u32[]{:S(2)}) copy-start(f32[1,5,128]{2,1,0:T(8,128)} %copy.385) | copy-start | bytes 7684 | tf_op jit(solution)/shard_map/while
  1007.5 13.8 %collective-permute-start.4 = (f32[5,128,128]{2,1,0:T(8,128)S(1)}, f32[5,128,128]{2,1,0:T(8,128)S(1)}, u32[]{:S(2)}, u32[]{:S(2)}) collective-permute-start(f32[5,128,128]{2,1,0:T(8,128)S(1)} %slice.791), channel_id=1, source_target_pairs={{0,16},{16,32},{32,48},{48,64},{64,80},{80,96},{96,112},{112,128},... | collective-permute-start | bytes 983048 | tf_op jit(solution)/shard_map/ppermute | solution.py:21
  (284 other events, 5810.3 us)
Sparse Core Ops, SparseCore 0:
  112.9 126.3 all-reduce.2
  889.2 117.2 all-reduce.4
where the time goes:
time: 1030 us
  local copies, waits for them, and re-layouts  334 us (32%)
  waiting for transfers between devices  321 us (31%)
  other arithmetic  318 us (31%)
  starting transfers between devices  20.2 us (2%)
  between operations  14.4 us (1%)
  loops' own time  12.5 us (1%)
    reduce_sum x40, other arithmetic, flux_tile(): jnp.sum(pair_scale * face_flux, axis=1)  246 us
    psum x2, waiting for transfers between devices, settle(): partial_value = lax.psum(partial_value, 'sub')  244 us
    while x1648, local copies, waits for them, and re-layouts  234 us
    ppermute x5, waiting for transfers between devices, shifted(): lax.ppermute(shard, axis, [(i, (i + by) % peers) for i in range(peers)])  77.5 us
    reduce_sum x16, other arithmetic, moment_tile(): col_sums = jnp.stack([jnp.sum(summand, axis=1) for summand in summands])  29.6 us
  transfers between devices with their start and end apart: 7, of which 6 were waited for; matrix products, arithmetic and copies ran while one was open for 1% of the time, Pallas kernels for 0%

commit v1 on v0

--- a/solution.py
+++ b/solution.py
@@ -318,7 +318,11 @@
 
     def settle(partial_value):
         row_count = partial_value.shape[0]
-        partial_value = lax.psum(partial_value, "sub")
+        partial_value = partial_value
+        for hop in (1, 2, 4, 8):
+            partial_value = partial_value + lax.ppermute(
+                partial_value, "sub", [(dev, dev ^ hop) for dev in range(16)]
+            )
         own_part = partial_value[:, :slab_leaves]
         next_part = partial_value[:, slab_leaves:]
         returned = shifted(next_part, "slab", 1)

time: 1030 us -> 1200 us (1.17)
  waiting for transfers between devices: 321 us -> 473 us
  starting transfers between devices: 20.2 us -> 51.6 us
  between operations: 14.4 us -> 1.08 us
    ppermute x0 -> x8, waiting for transfers between devices: none -> 395 us  [settle(): lax.ppermute(partial_value, 'sub', [(dev, dev ^ hop) for dev in range(16)])]
    psum x2 -> x0, waiting for transfers between devices: 244 us -> none  [settle(): partial_value = lax.psum(partial_value, 'sub')]
    ppermute x0 -> x8, starting transfers between devices: none -> 33.2 us  [settle(): lax.ppermute(partial_value, 'sub', [(dev, dev ^ hop) for dev in range(16)])]
    while x1648 -> x1632, local copies, waits for them, and re-layouts: 234 us -> 239 us
  transfers between devices with their start and end apart: 7 -> 13, of which waited for: 6 -> 12; matrix products, arithmetic and copies ran while one was open for 1% -> 1% of each run, Pallas kernels for 0% -> 0%
where the time goes in v1:
time: 1200 us
  waiting for transfers between devices  473 us (39%)
  local copies, waits for them, and re-layouts  337 us (28%)
  other arithmetic  315 us (26%)
  starting transfers between devices  51.6 us (4%)
  loops' own time  12.1 us (1%)
    ppermute x8, waiting for transfers between devices, settle(): lax.ppermute(partial_value, 'sub', [(dev, dev ^ hop) for dev in range(16)])  395 us
    reduce_sum x40, other arithmetic, flux_tile(): jnp.sum(pair_scale * face_flux, axis=1)  244 us
    while x1632, local copies, waits for them, and re-layouts  239 us
    ppermute x5, waiting for transfers between devices, shifted(): lax.ppermute(shard, axis, [(i, (i + by) % peers) for i in range(peers)])  77.4 us
    ppermute x8, starting transfers between devices, settle(): lax.ppermute(partial_value, 'sub', [(dev, dev ^ hop) for dev in range(16)])  33.2 us
    reduce_sum x16, other arithmetic, moment_tile(): col_sums = jnp.stack([jnp.sum(summand, axis=1) for summand in summands])  29.5 us
  transfers between devices with their start and end apart: 13, of which 12 were waited for; matrix products, arithmetic and copies ran while one was open for 1% of the time, Pallas kernels for 0%

profile of v1, /device:TPU:1, one launch (start us, length us, event | category | flops | bytes accessed | tf_op | source)
XLA Modules:
  0.0 1196.5 jit_solution(10769122998254877427)
XLA Ops:
  0.7 8.1 collective-permute-start.1
  21.4 3.2 collective-permute-done
  25.8 73.7 %while.30 = (s32[]{:T(128)}, f32[22,40,128]{2,1,0:T(8,128)S(1)}, f32[22,40,128]{2,1,0:T(8,128)S(1)}, s32[]{:T(128)}, s32[40]{0:T(128)}, /*index=5*/f32[8,256,128...) while((s32[]{:T(128)}, f32[22,40,128]{2,1,0:T(8,128)S(1)}, ...), condition=%wide.region_47.49_spmd.clone, body=%wide.region_2.48_spmd.clone.sunk | while | flops 9721420 | bytes 1241347 | solution.py:313
  30.4 2.9 fusion.246
  39.7 2.9 fusion.246
  48.9 2.9 fusion.246
  58.1 2.9 fusion.246
  67.3 2.9 fusion.246
  85.8 2.9 fusion.246
  105.7 5.2 collective-permute-done.2
  113.3 63.9 %collective-permute-done.3 = f32[22,256,128]{2,1,0:T(8,128)S(1)} collective-permute-done((f32[22,256,128]{2,1,0:T(8,128)S(1)}, f32[22,256,128]{2,1,0:T(8,128)S(1)}, u32[]{:S(2)}, u32[]{:S(2)}) %collective-permute-start.3) | collective-permute-done | bytes 2883616 | tf_op jit(solution)/shard_map/ppermute | solution.py:323
  177.6 5.8 collective-permute-start.4
  183.4 124.7 %collective-permute-done.4 = f32[22,256,128]{2,1,0:T(8,128)S(1)} collective-permute-done((f32[22,256,128]{2,1,0:T(8,128)S(1)}, f32[22,256,128]{2,1,0:T(8,128)S(1)}, u32[]{:S(2)}, u32[]{:S(2)}) %collective-permute-start.4) | collective-permute-done | bytes 2883616 | tf_op jit(solution)/shard_map/ppermute | solution.py:323
  308.5 9.1 collective-permute-start.5
  317.6 123.9 %collective-permute-done.5 = f32[22,256,128]{2,1,0:T(8,128)S(1)} collective-permute-done((f32[22,256,128]{2,1,0:T(8,128)S(1)}, f32[22,256,128]{2,1,0:T(8,128)S(1)}, u32[]{:S(2)}, u32[]{:S(2)}) %collective-permute-start.5) | collective-permute-done | bytes 2883616 | tf_op jit(solution)/shard_map/ppermute | solution.py:323
  442.1 3.4 collective-permute-start.6
  445.5 32.9 %collective-permute-done.6 = f32[22,128,128]{2,1,0:T(8,128)S(1)} collective-permute-done((f32[22,128,128]{2,1,0:T(8,128)S(1)}, f32[22,128,128]{2,1,0:T(8,128)S(1)}, u32[]{:S(2)}, u32[]{:S(2)}) %collective-permute-start.6) | collective-permute-done | bytes 1441824 | tf_op jit(solution)/shard_map/ppermute | solution.py:21
  482.1 29.6 %collective-permute-done.7 = f32[22,128,128]{2,1,0:T(8,128)S(1)} collective-permute-done((f32[22,128,128]{2,1,0:T(8,128)S(1)}, f32[22,128,128]{2,1,0:T(8,128)S(1)}, u32[]{:S(2)}, u32[]{:S(2)}) %collective-permute-start.7) | collective-permute-done | bytes 1441824 | tf_op jit(solution)/shard_map/ppermute | solution.py:21
  514.3 572.5 %while.31 = (s32[]{:T(128)}, f32[5,40,128]{2,1,0:T(8,128)}, f32[5,40,128]{2,1,0:T(8,128)S(1)}, s32[]{:T(128)}, s32[40]{0:T(128)}, /*index=5*/f32[8,256,128]{2,0,...) while((s32[]{:T(128)}, f32[5,40,128]{2,1,0:T(8,128)}, ...), condition=%wide.region_59.62_spmd.clone, body=%wide.region_48.61_spmd.clone.sunk | while | flops 113486544 | bytes 2750965 | solution.py:313
  553.3 6.3 fusion.254
  559.6 5.9 fusion.253
  565.6 6.2 fusion.255
  572.1 5.5 fusion.256
  577.6 6.7 fusion.257
  624.8 6.3 fusion.254
  631.2 5.9 fusion.253
  637.1 6.2 fusion.255
  643.7 5.5 fusion.256
  649.2 6.7 fusion.257
  696.4 6.3 fusion.254
  702.8 5.9 fusion.253
  708.7 6.2 fusion.255
  715.2 5.5 fusion.256
  720.7 6.7 fusion.257
  767.9 6.3 fusion.254
  774.3 5.9 fusion.253
  780.2 6.2 fusion.255
  786.8 5.5 fusion.256
  792.3 6.7 fusion.257
  839.5 6.3 fusion.254
  845.9 5.9 fusion.253
  851.8 6.2 fusion.255
  858.3 5.5 fusion.256
  863.8 6.7 fusion.257
  911.1 6.3 fusion.254
  917.4 5.9 fusion.253
  923.4 6.2 fusion.255
  929.9 5.5 fusion.256
  935.4 6.7 fusion.257
  982.6 6.3 fusion.254
  989.0 5.9 fusion.253
  994.9 6.2 fusion.255
  1001.5 5.5 fusion.256
  1007.0 6.7 fusion.257
  1054.2 6.3 fusion.254
  1060.6 5.9 fusion.253
  1066.5 6.2 fusion.255
  1073.0 5.5 fusion.256
  1078.5 6.7 fusion.257
  1095.4 16.1 %collective-permute-done.9 = f32[5,256,128]{2,1,0:T(8,128)S(1)} collective-permute-done((f32[5,256,128]{2,1,0:T(8,128)S(1)}, f32[5,256,128]{2,1,0:T(8,128)S(1)}, u32[]{:S(2)}, u32[]{:S(2)}) %collective-permute-start.9) | collective-permute-done | bytes 655392 | tf_op jit(solution)/shard_map/ppermute | solution.py:323
  1113.6 31.6 %collective-permute-done.10 = f32[5,256,128]{2,1,0:T(8,128)S(1)} collective-permute-done((f32[5,256,128]{2,1,0:T(8,128)S(1)}, f32[5,256,128]{2,1,0:T(8,128)S(1)}, u32[]{:S(2)}, u32[]{:S(2)}) %collective-permute-start.10) | collective-permute-done | bytes 655392 | tf_op jit(solution)/shard_map/ppermute | solution.py:323
  1145.2 8.7 collective-permute-start.11
  1153.9 27.9 %collective-permute-done.11 = f32[5,256,128]{2,1,0:T(8,128)S(1)} collective-permute-done((f32[5,256,128]{2,1,0:T(8,128)S(1)}, f32[5,256,128]{2,1,0:T(8,128)S(1)}, u32[]{:S(2)}, u32[]{:S(2)}) %collective-permute-start.11) | collective-permute-done | bytes 655392 | tf_op jit(solution)/shard_map/ppermute | solution.py:323
  1183.8 11.6 collective-permute-done.12
  (2204 shorter events, 415.9 us)
Async XLA Ops:
  0.7 20.0 %collective-permute-start.1 = (f32[128]{0:T(128)S(1)}, f32[128]{0:T(128)S(1)}, u32[]{:S(2)}, u32[]{:S(2)}) collective-permute-start(f32[128]{0:T(128)S(1)} %convert_element_type.36), channel_id=1, source_target_pairs={{0,496},{16,0},{32,16},{48,32},{64,48},{80,64},{96,80},{112,96},{1... | collective-permute-start | bytes 1544 | tf_op jit(solution)/shard_map/ppermute | solution.py:21
  10.2 14.4 %collective-permute-start = (f32[8,16384]{1,0:T(8,128)S(1)}, f32[8,16384]{1,0:T(8,128)S(1)}, u32[]{:S(2)}, u32[]{:S(2)}) collective-permute-start(f32[8,16384]{1,0:T(8,128)S(1)} %pad_maximum_fusion.2), channel_id=1, source_target_pairs={{0,496},{16,0},{32,16},{48,32},{64,48},{80,64},{96,80},{112,96},{1... | collective-permute-start | bytes 1572872 | tf_op jit(solution)/shard_map/ppermute | solution.py:21
  103.8 7.2 collective-permute-start.2
  111.4 65.8 %collective-permute-start.3 = (f32[22,256,128]{2,1,0:T(8,128)S(1)}, f32[22,256,128]{2,1,0:T(8,128)S(1)}, u32[]{:S(2)}, u32[]{:S(2)}) collective-permute-start(f32[22,256,128]{2,1,0:T(8,128)S(1)} %add.914), channel_id=1, source_target_pairs={{0,2},{1,3},{2,0},{3,1},{4,6},{5,7},{6,4},{7,5},{8,10},{9,11},{10,... | collective-permute-start | bytes 8650760 | tf_op jit(solution)/shard_map/ppermute | solution.py:323
  177.6 130.5 %collective-permute-start.4 = (f32[22,256,128]{2,1,0:T(8,128)S(1)}, f32[22,256,128]{2,1,0:T(8,128)S(1)}, u32[]{:S(2)}, u32[]{:S(2)}) collective-permute-start(f32[22,256,128]{2,1,0:T(8,128)S(1)} %add.915), channel_id=1, source_target_pairs={{0,4},{1,5},{2,6},{3,7},{4,0},{5,1},{6,2},{7,3},{8,12},{9,13},{10,... | collective-permute-start | bytes 8650760 | tf_op jit(solution)/shard_map/ppermute | solution.py:323
  308.5 133.1 %collective-permute-start.5 = (f32[22,256,128]{2,1,0:T(8,128)S(1)}, f32[22,256,128]{2,1,0:T(8,128)S(1)}, u32[]{:S(2)}, u32[]{:S(2)}) collective-permute-start(f32[22,256,128]{2,1,0:T(8,128)S(1)} %add.916), channel_id=1, source_target_pairs={{0,8},{1,9},{2,10},{3,11},{4,12},{5,13},{6,14},{7,15},{8,0},{9,1},... | collective-permute-start | bytes 8650760 | tf_op jit(solution)/shard_map/ppermute | solution.py:323
  442.1 36.3 %collective-permute-start.6 = (f32[22,128,128]{2,1,0:T(8,128)S(1)}, f32[22,128,128]{2,1,0:T(8,128)S(1)}, u32[]{:S(2)}, u32[]{:S(2)}) collective-permute-start(f32[22,128,128]{2,1,0:T(8,128)S(1)} %slice.766), channel_id=1, source_target_pairs={{0,16},{16,32},{32,48},{48,64},{64,80},{80,96},{96,112},{112,128},... | collective-permute-start | bytes 4325384 | tf_op jit(solution)/shard_map/ppermute | solution.py:21
  479.6 32.1 %collective-permute-start.7 = (f32[22,128,128]{2,1,0:T(8,128)S(1)}, f32[22,128,128]{2,1,0:T(8,128)S(1)}, u32[]{:S(2)}, u32[]{:S(2)}) collective-permute-start(f32[22,128,128]{2,1,0:T(8,128)S(1)} %bitcast_dynamic-update-slice_fusion), channel_id=1, source_target_pairs={{0,496},{16,0},{32,16},{48,32},{64,48},{80,64},{96,80},{112,96},{1... | collective-permute-start | bytes 4325384 | tf_op jit(solution)/shard_map/ppermute | solution.py:21
  530.1 29.5 %copy-start.5 = (f32[1,5,128]{2,1,0:T(8,128)S(1)}, f32[1,5,128]{2,1,0:T(8,128)}, u32[]{:S(2)}) copy-start(f32[1,5,128]{2,1,0:T(8,128)} %copy.379) | copy-start | bytes 7684 | tf_op jit(solution)/shard_map/while
  530.1 29.5 %copy-start.6 = (f32[1,5,128]{2,1,0:T(8,128)S(1)}, f32[1,5,128]{2,1,0:T(8,128)}, u32[]{:S(2)}) copy-start(f32[1,5,128]{2,1,0:T(8,128)} %copy.380) | copy-start | bytes 7684 | tf_op jit(solution)/shard_map/while
  530.1 29.5 %copy-start.7 = (f32[1,5,128]{2,1,0:T(8,128)S(1)}, f32[1,5,128]{2,1,0:T(8,128)}, u32[]{:S(2)}) copy-start(f32[1,5,128]{2,1,0:T(8,128)} %copy.381) | copy-start | bytes 7684 | tf_op jit(solution)/shard_map/while
  530.1 29.5 %copy-start.8 = (f32[1,5,128]{2,1,0:T(8,128)S(1)}, f32[1,5,128]{2,1,0:T(8,128)}, u32[]{:S(2)}) copy-start(f32[1,5,128]{2,1,0:T(8,128)} %copy.384) | copy-start | bytes 7684 | tf_op jit(solution)/shard_map/while
  530.1 29.5 %copy-start.9 = (f32[1,5,128]{2,1,0:T(8,128)S(1)}, f32[1,5,128]{2,1,0:T(8,128)}, u32[]{:S(2)}) copy-start(f32[1,5,128]{2,1,0:T(8,128)} %copy.385) | copy-start | bytes 7684 | tf_op jit(solution)/shard_map/while
  530.2 29.5 %copy-start.10 = (f32[1,5,128]{2,1,0:T(8,128)S(1)}, f32[1,5,128]{2,1,0:T(8,128)}, u32[]{:S(2)}) copy-start(f32[1,5,128]{2,1,0:T(8,128)} %copy.386) | copy-start | bytes 7684 | tf_op jit(solution)/shard_map/while
  530.2 29.5 %copy-start.11 = (f32[1,5,128]{2,1,0:T(8,128)S(1)}, f32[1,5,128]{2,1,0:T(8,128)}, u32[]{:S(2)}) copy-start(f32[1,5,128]{2,1,0:T(8,128)} %copy.389) | copy-start | bytes 7684 | tf_op jit(solution)/shard_map/while
  530.2 29.5 %copy-start.12 = (f32[1,5,128]{2,1,0:T(8,128)S(1)}, f32[1,5,128]{2,1,0:T(8,128)}, u32[]{:S(2)}) copy-start(f32[1,5,128]{2,1,0:T(8,128)} %copy.390) | copy-start | bytes 7684 | tf_op jit(solution)/shard_map/while
  601.7 29.5 %copy-start.5 = (f32[1,5,128]{2,1,0:T(8,128)S(1)}, f32[1,5,128]{2,1,0:T(8,128)}, u32[]{:S(2)}) copy-start(f32[1,5,128]{2,1,0:T(8,128)} %copy.379) | copy-start | bytes 7684 | tf_op jit(solution)/shard_map/while
  601.7 29.5 %copy-start.6 = (f32[1,5,128]{2,1,0:T(8,128)S(1)}, f32[1,5,128]{2,1,0:T(8,128)}, u32[]{:S(2)}) copy-start(f32[1,5,128]{2,1,0:T(8,128)} %copy.380) | copy-start | bytes 7684 | tf_op jit(solution)/shard_map/while
  601.7 29.5 %copy-start.7 = (f32[1,5,128]{2,1,0:T(8,128)S(1)}, f32[1,5,128]{2,1,0:T(8,128)}, u32[]{:S(2)}) copy-start(f32[1,5,128]{2,1,0:T(8,128)} %copy.381) | copy-start | bytes 7684 | tf_op jit(solution)/shard_map/while
  601.7 29.5 %copy-start.8 = (f32[1,5,128]{2,1,0:T(8,128)S(1)}, f32[1,5,128]{2,1,0:T(8,128)}, u32[]{:S(2)}) copy-start(f32[1,5,128]{2,1,0:T(8,128)} %copy.384) | copy-start | bytes 7684 | tf_op jit(solution)/shard_map/while
  601.7 29.5 %copy-start.9 = (f32[1,5,128]{2,1,0:T(8,128)S(1)}, f32[1,5,128]{2,1,0:T(8,128)}, u32[]{:S(2)}) copy-start(f32[1,5,128]{2,1,0:T(8,128)} %copy.385) | copy-start | bytes 7684 | tf_op jit(solution)/shard_map/while
  601.7 29.5 %copy-start.10 = (f32[1,5,128]{2,1,0:T(8,128)S(1)}, f32[1,5,128]{2,1,0:T(8,128)}, u32[]{:S(2)}) copy-start(f32[1,5,128]{2,1,0:T(8,128)} %copy.386) | copy-start | bytes 7684 | tf_op jit(solution)/shard_map/while
  601.7 29.5 %copy-start.11 = (f32[1,5,128]{2,1,0:T(8,128)S(1)}, f32[1,5,128]{2,1,0:T(8,128)}, u32[]{:S(2)}) copy-start(f32[1,5,128]{2,1,0:T(8,128)} %copy.389) | copy-start | bytes 7684 | tf_op jit(solution)/shard_map/while
  601.7 29.5 %copy-start.12 = (f32[1,5,128]{2,1,0:T(8,128)S(1)}, f32[1,5,128]{2,1,0:T(8,128)}, u32[]{:S(2)}) copy-start(f32[1,5,128]{2,1,0:T(8,128)} %copy.390) | copy-start | bytes 7684 | tf_op jit(solution)/shard_map/while
  673.2 29.5 %copy-start.5 = (f32[1,5,128]{2,1,0:T(8,128)S(1)}, f32[1,5,128]{2,1,0:T(8,128)}, u32[]{:S(2)}) copy-start(f32[1,5,128]{2,1,0:T(8,128)} %copy.379) | copy-start | bytes 7684 | tf_op jit(solution)/shard_map/while
  673.2 29.5 %copy-start.6 = (f32[1,5,128]{2,1,0:T(8,128)S(1)}, f32[1,5,128]{2,1,0:T(8,128)}, u32[]{:S(2)}) copy-start(f32[1,5,128]{2,1,0:T(8,128)} %copy.380) | copy-start | bytes 7684 | tf_op jit(solution)/shard_map/while
  673.2 29.5 %copy-start.7 = (f32[1,5,128]{2,1,0:T(8,128)S(1)}, f32[1,5,128]{2,1,0:T(8,128)}, u32[]{:S(2)}) copy-start(f32[1,5,128]{2,1,0:T(8,128)} %copy.381) | copy-start | bytes 7684 | tf_op jit(solution)/shard_map/while
  673.3 29.5 %copy-start.8 = (f32[1,5,128]{2,1,0:T(8,128)S(1)}, f32[1,5,128]{2,1,0:T(8,128)}, u32[]{:S(2)}) copy-start(f32[1,5,128]{2,1,0:T(8,128)} %copy.384) | copy-start | bytes 7684 | tf_op jit(solution)/shard_map/while
  673.3 29.5 %copy-start.9 = (f32[1,5,128]{2,1,0:T(8,128)S(1)}, f32[1,5,128]{2,1,0:T(8,128)}, u32[]{:S(2)}) copy-start(f32[1,5,128]{2,1,0:T(8,128)} %copy.385) | copy-start | bytes 7684 | tf_op jit(solution)/shard_map/while
  673.3 29.5 %copy-start.10 = (f32[1,5,128]{2,1,0:T(8,128)S(1)}, f32[1,5,128]{2,1,0:T(8,128)}, u32[]{:S(2)}) copy-start(f32[1,5,128]{2,1,0:T(8,128)} %copy.386) | copy-start | bytes 7684 | tf_op jit(solution)/shard_map/while
  673.3 29.5 %copy-start.11 = (f32[1,5,128]{2,1,0:T(8,128)S(1)}, f32[1,5,128]{2,1,0:T(8,128)}, u32[]{:S(2)}) copy-start(f32[1,5,128]{2,1,0:T(8,128)} %copy.389) | copy-start | bytes 7684 | tf_op jit(solution)/shard_map/while
  673.3 29.5 %copy-start.12 = (f32[1,5,128]{2,1,0:T(8,128)S(1)}, f32[1,5,128]{2,1,0:T(8,128)}, u32[]{:S(2)}) copy-start(f32[1,5,128]{2,1,0:T(8,128)} %copy.390) | copy-start | bytes 7684 | tf_op jit(solution)/shard_map/while
  744.8 29.5 %copy-start.5 = (f32[1,5,128]{2,1,0:T(8,128)S(1)}, f32[1,5,128]{2,1,0:T(8,128)}, u32[]{:S(2)}) copy-start(f32[1,5,128]{2,1,0:T(8,128)} %copy.379) | copy-start | bytes 7684 | tf_op jit(solution)/shard_map/while
  744.8 29.5 %copy-start.6 = (f32[1,5,128]{2,1,0:T(8,128)S(1)}, f32[1,5,128]{2,1,0:T(8,128)}, u32[]{:S(2)}) copy-start(f32[1,5,128]{2,1,0:T(8,128)} %copy.380) | copy-start | bytes 7684 | tf_op jit(solution)/shard_map/while
  744.8 29.5 %copy-start.7 = (f32[1,5,128]{2,1,0:T(8,128)S(1)}, f32[1,5,128]{2,1,0:T(8,128)}, u32[]{:S(2)}) copy-start(f32[1,5,128]{2,1,0:T(8,128)} %copy.381) | copy-start | bytes 7684 | tf_op jit(solution)/shard_map/while
  744.8 29.5 %copy-start.8 = (f32[1,5,128]{2,1,0:T(8,128)S(1)}, f32[1,5,128]{2,1,0:T(8,128)}, u32[]{:S(2)}) copy-start(f32[1,5,128]{2,1,0:T(8,128)} %copy.384) | copy-start | bytes 7684 | tf_op jit(solution)/shard_map/while
  744.8 29.5 %copy-start.9 = (f32[1,5,128]{2,1,0:T(8,128)S(1)}, f32[1,5,128]{2,1,0:T(8,128)}, u32[]{:S(2)}) copy-start(f32[1,5,128]{2,1,0:T(8,128)} %copy.385) | copy-start | bytes 7684 | tf_op jit(solution)/shard_map/while
  744.8 29.5 %copy-start.10 = (f32[1,5,128]{2,1,0:T(8,128)S(1)}, f32[1,5,128]{2,1,0:T(8,128)}, u32[]{:S(2)}) copy-start(f32[1,5,128]{2,1,0:T(8,128)} %copy.386) | copy-start | bytes 7684 | tf_op jit(solution)/shard_map/while
  744.8 29.5 %copy-start.11 = (f32[1,5,128]{2,1,0:T(8,128)S(1)}, f32[1,5,128]{2,1,0:T(8,128)}, u32[]{:S(2)}) copy-start(f32[1,5,128]{2,1,0:T(8,128)} %copy.389) | copy-start | bytes 7684 | tf_op jit(solution)/shard_map/while
  744.9 29.5 %copy-start.12 = (f32[1,5,128]{2,1,0:T(8,128)S(1)}, f32[1,5,128]{2,1,0:T(8,128)}, u32[]{:S(2)}) copy-start(f32[1,5,128]{2,1,0:T(8,128)} %copy.390) | copy-start | bytes 7684 | tf_op jit(solution)/shard_map/while
  816.3 29.5 %copy-start.5 = (f32[1,5,128]{2,1,0:T(8,128)S(1)}, f32[1,5,128]{2,1,0:T(8,128)}, u32[]{:S(2)}) copy-start(f32[1,5,128]{2,1,0:T(8,128)} %copy.379) | copy-start | bytes 7684 | tf_op jit(solution)/shard_map/while
  816.4 29.5 %copy-start.6 = (f32[1,5,128]{2,1,0:T(8,128)S(1)}, f32[1,5,128]{2,1,0:T(8,128)}, u32[]{:S(2)}) copy-start(f32[1,5,128]{2,1,0:T(8,128)} %copy.380) | copy-start | bytes 7684 | tf_op jit(solution)/shard_map/while
  816.4 29.5 %copy-start.7 = (f32[1,5,128]{2,1,0:T(8,128)S(1)}, f32[1,5,128]{2,1,0:T(8,128)}, u32[]{:S(2)}) copy-start(f32[1,5,128]{2,1,0:T(8,128)} %copy.381) | copy-start | bytes 7684 | tf_op jit(solution)/shard_map/while
  887.9 29.5 %copy-start.5 = (f32[1,5,128]{2,1,0:T(8,128)S(1)}, f32[1,5,128]{2,1,0:T(8,128)}, u32[]{:S(2)}) copy-start(f32[1,5,128]{2,1,0:T(8,128)} %copy.379) | copy-start | bytes 7684 | tf_op jit(solution)/shard_map/while
  887.9 29.5 %copy-start.6 = (f32[1,5,128]{2,1,0:T(8,128)S(1)}, f32[1,5,128]{2,1,0:T(8,128)}, u32[]{:S(2)}) copy-start(f32[1,5,128]{2,1,0:T(8,128)} %copy.380) | copy-start | bytes 7684 | tf_op jit(solution)/shard_map/while
  887.9 29.5 %copy-start.7 = (f32[1,5,128]{2,1,0:T(8,128)S(1)}, f32[1,5,128]{2,1,0:T(8,128)}, u32[]{:S(2)}) copy-start(f32[1,5,128]{2,1,0:T(8,128)} %copy.381) | copy-start | bytes 7684 | tf_op jit(solution)/shard_map/while
  887.9 29.5 %copy-start.8 = (f32[1,5,128]{2,1,0:T(8,128)S(1)}, f32[1,5,128]{2,1,0:T(8,128)}, u32[]{:S(2)}) copy-start(f32[1,5,128]{2,1,0:T(8,128)} %copy.384) | copy-start | bytes 7684 | tf_op jit(solution)/shard_map/while
  887.9 29.5 %copy-start.9 = (f32[1,5,128]{2,1,0:T(8,128)S(1)}, f32[1,5,128]{2,1,0:T(8,128)}, u32[]{:S(2)}) copy-start(f32[1,5,128]{2,1,0:T(8,128)} %copy.385) | copy-start | bytes 7684 | tf_op jit(solution)/shard_map/while
  888.0 29.5 %copy-start.10 = (f32[1,5,128]{2,1,0:T(8,128)S(1)}, f32[1,5,128]{2,1,0:T(8,128)}, u32[]{:S(2)}) copy-start(f32[1,5,128]{2,1,0:T(8,128)} %copy.386) | copy-start | bytes 7684 | tf_op jit(solution)/shard_map/while
  888.0 29.5 %copy-start.11 = (f32[1,5,128]{2,1,0:T(8,128)S(1)}, f32[1,5,128]{2,1,0:T(8,128)}, u32[]{:S(2)}) copy-start(f32[1,5,128]{2,1,0:T(8,128)} %copy.389) | copy-start | bytes 7684 | tf_op jit(solution)/shard_map/while
  888.0 29.5 %copy-start.12 = (f32[1,5,128]{2,1,0:T(8,128)S(1)}, f32[1,5,128]{2,1,0:T(8,128)}, u32[]{:S(2)}) copy-start(f32[1,5,128]{2,1,0:T(8,128)} %copy.390) | copy-start | bytes 7684 | tf_op jit(solution)/shard_map/while
  959.5 29.5 %copy-start.5 = (f32[1,5,128]{2,1,0:T(8,128)S(1)}, f32[1,5,128]{2,1,0:T(8,128)}, u32[]{:S(2)}) copy-start(f32[1,5,128]{2,1,0:T(8,128)} %copy.379) | copy-start | bytes 7684 | tf_op jit(solution)/shard_map/while
  959.5 29.5 %copy-start.6 = (f32[1,5,128]{2,1,0:T(8,128)S(1)}, f32[1,5,128]{2,1,0:T(8,128)}, u32[]{:S(2)}) copy-start(f32[1,5,128]{2,1,0:T(8,128)} %copy.380) | copy-start | bytes 7684 | tf_op jit(solution)/shard_map/while
  959.5 29.5 %copy-start.7 = (f32[1,5,128]{2,1,0:T(8,128)S(1)}, f32[1,5,128]{2,1,0:T(8,128)}, u32[]{:S(2)}) copy-start(f32[1,5,128]{2,1,0:T(8,128)} %copy.381) | copy-start | bytes 7684 | tf_op jit(solution)/shard_map/while
  959.5 29.5 %copy-start.8 = (f32[1,5,128]{2,1,0:T(8,128)S(1)}, f32[1,5,128]{2,1,0:T(8,128)}, u32[]{:S(2)}) copy-start(f32[1,5,128]{2,1,0:T(8,128)} %copy.384) | copy-start | bytes 7684 | tf_op jit(solution)/shard_map/while
  959.5 29.5 %copy-start.9 = (f32[1,5,128]{2,1,0:T(8,128)S(1)}, f32[1,5,128]{2,1,0:T(8,128)}, u32[]{:S(2)}) copy-start(f32[1,5,128]{2,1,0:T(8,128)} %copy.385) | copy-start | bytes 7684 | tf_op jit(solution)/shard_map/while
  959.5 29.5 %copy-start.10 = (f32[1,5,128]{2,1,0:T(8,128)S(1)}, f32[1,5,128]{2,1,0:T(8,128)}, u32[]{:S(2)}) copy-start(f32[1,5,128]{2,1,0:T(8,128)} %copy.386) | copy-start | bytes 7684 | tf_op jit(solution)/shard_map/while
  959.5 29.5 %copy-start.11 = (f32[1,5,128]{2,1,0:T(8,128)S(1)}, f32[1,5,128]{2,1,0:T(8,128)}, u32[]{:S(2)}) copy-start(f32[1,5,128]{2,1,0:T(8,128)} %copy.389) | copy-start | bytes 7684 | tf_op jit(solution)/shard_map/while
  959.5 29.5 %copy-start.12 = (f32[1,5,128]{2,1,0:T(8,128)S(1)}, f32[1,5,128]{2,1,0:T(8,128)}, u32[]{:S(2)}) copy-start(f32[1,5,128]{2,1,0:T(8,128)} %copy.390) | copy-start | bytes 7684 | tf_op jit(solution)/shard_map/while
  1089.4 4.0 collective-permute-start.8
  1093.5 18.0 %collective-permute-start.9 = (f32[5,256,128]{2,1,0:T(8,128)S(1)}, f32[5,256,128]{2,1,0:T(8,128)S(1)}, u32[]{:S(2)}, u32[]{:S(2)}) collective-permute-start(f32[5,256,128]{2,1,0:T(8,128)S(1)} %add.958), channel_id=1, source_target_pairs={{0,2},{1,3},{2,0},{3,1},{4,6},{5,7},{6,4},{7,5},{8,10},{9,11},{10,... | collective-permute-start | bytes 1966088 | tf_op jit(solution)/shard_map/ppermute | solution.py:323
  1111.6 33.5 %collective-permute-start.10 = (f32[5,256,128]{2,1,0:T(8,128)S(1)}, f32[5,256,128]{2,1,0:T(8,128)S(1)}, u32[]{:S(2)}, u32[]{:S(2)}) collective-permute-start(f32[5,256,128]{2,1,0:T(8,128)S(1)} %add.959), channel_id=1, source_target_pairs={{0,4},{1,5},{2,6},{3,7},{4,0},{5,1},{6,2},{7,3},{8,12},{9,13},{10,... | collective-permute-start | bytes 1966088 | tf_op jit(solution)/shard_map/ppermute | solution.py:323
  1145.2 36.6 %collective-permute-start.11 = (f32[5,256,128]{2,1,0:T(8,128)S(1)}, f32[5,256,128]{2,1,0:T(8,128)S(1)}, u32[]{:S(2)}, u32[]{:S(2)}) collective-permute-start(f32[5,256,128]{2,1,0:T(8,128)S(1)} %add.960), channel_id=1, source_target_pairs={{0,8},{1,9},{2,10},{3,11},{4,12},{5,13},{6,14},{7,15},{8,0},{9,1},... | collective-permute-start | bytes 1966088 | tf_op jit(solution)/shard_map/ppermute | solution.py:323
  1181.9 13.5 %collective-permute-start.12 = (f32[5,128,128]{2,1,0:T(8,128)S(1)}, f32[5,128,128]{2,1,0:T(8,128)S(1)}, u32[]{:S(2)}, u32[]{:S(2)}) collective-permute-start(f32[5,128,128]{2,1,0:T(8,128)S(1)} %slice.791), channel_id=1, source_target_pairs={{0,16},{16,32},{32,48},{48,64},{64,80},{80,96},{96,112},{112,128},... | collective-permute-start | bytes 983048 | tf_op jit(solution)/shard_map/ppermute | solution.py:21
  (281 other events, 5695.7 us)
